TPU v7x, 128 devices: a whole 4x4x4 slice. The times are simulated.
128 devices in a mesh: ep: 4 (over x), tm: 32 (over y, z, core).
Axes of the slice: x: 4, y: 4, z: 4, core: 2. Of those that a mesh axis runs over, the one named last changes fastest.
Arguments:
- predictions: float32 [128, 1048576], P('ep', 'tm'), may hold values from -6 to 6
- leaf_index: int32 [128, 1048576], P('ep', 'tm'), may hold values from 0 to 63
- events: int32 [128, 1048576], P('ep', 'tm'), may hold values 0 or 1
- tie_start: int32 [1048576], P('tm'), may hold values from 0 to 1, as said below
Outputs:
- new_pred: float32 [128, 1048576], P('ep', 'tm')
- leaf_weights: float32 [128, 64], P('ep')
- grad_hess: bfloat16 [2, 128, 32, 32768], P(None, None, 'tm', 'ep')
Inputs may be any that keep to these rules, and one draw needn't show every extreme that they name: `tie_start`: every row whose index is a multiple of 128 begins a tie group.
All inputs are finite; a program needn't handle non-finite values. No bound on the sum of `events` on one device may be relied on, other than what follows from the above.
Results may differ from a plain program's by a relative error of at most 0.0023.
Values may be sent and summed in bfloat16 or wider, within the bound.
A program may use at most 128 MiB of HBM per device.

v0:
```python
import math
import jax
import jax.numpy as jnp
from jax import lax
from jax.sharding import PartitionSpec as P

LEAVES = 64


def prefix(part, axis, combine, identity, reverse):
    count = lax.axis_size(axis)
    place = lax.axis_index(axis)
    ahead = count - 1 - place if reverse else place
    gathered = jax.tree.map(lambda a: lax.all_gather(a, axis), part)
    state = jax.tree.map(lambda a, e: jnp.zeros_like(a) + jnp.asarray(e, a.dtype), part, identity)

    def one(turn, state):
        source = count - 1 - turn if reverse else turn
        return combine(
            state, jax.tree.map(lambda a: lax.dynamic_index_in_dim(a, source, 0, False), gathered)
        )

    return lax.fori_loop(0, ahead, one, state)


def tile_matrices(tie_start):
    length = tie_start.shape[0]
    blocks = length // 128
    starts = tie_start.reshape(blocks, 128)
    labels = jnp.arange(128, dtype=jnp.int32)
    first_local = lax.cummax(jnp.where(starts == 1, labels[None, :], 0), axis=1)
    next_start = jnp.concatenate([starts[:, 1:], jnp.ones((blocks, 1), jnp.int32)], axis=1)
    last_local = lax.cummin(jnp.where(next_start == 1, labels[None, :], 127), axis=1, reverse=True)
    backward = (labels[None, :, None] >= first_local[:, None, :]).astype(jnp.float32)
    forward = (labels[None, :, None] <= last_local[:, None, :]).astype(jnp.float32)
    return (backward, forward)


def block_cumsum(values, matrices, from_end):
    groups = values.shape[0]
    length = values.shape[1]
    blocks = length // 128
    shaped = values.reshape(groups, blocks, 128)
    within = jnp.einsum("ebj,bji->ebi", shaped, matrices, precision=lax.Precision.HIGHEST)
    totals = jnp.sum(shaped, axis=2)
    if from_end:
        offsets = jnp.cumsum(totals[:, ::-1], axis=1)[:, ::-1] - totals
    else:
        offsets = jnp.cumsum(totals, axis=1) - totals
    return (within + offsets[:, :, None]).reshape(groups, length)


def add_values(earlier, later):
    return jax.tree.map(lambda left, right: left + right, earlier, later)


def leaf_partials(leaf_index, gradient, hessian, leaves):
    length = leaf_index.shape[1]
    width = math.gcd(length, 2048)
    labels = jnp.arange(leaves, dtype=jnp.int32)

    def one_block(step, totals):
        start = step * width
        part_leaf = lax.dynamic_slice_in_dim(leaf_index, start, width, 1)
        part_grad = lax.dynamic_slice_in_dim(gradient, start, width, 1)
        part_hess = lax.dynamic_slice_in_dim(hessian, start, width, 1)
        hits = part_leaf[:, None, :] == labels[None, :, None]
        gsum = jnp.sum(jnp.where(hits, part_grad[:, None, :], 0.0), axis=2)
        hsum = jnp.sum(jnp.where(hits, part_hess[:, None, :], 0.0), axis=2)
        return totals + jnp.stack([gsum, hsum], axis=1)

    empty = jnp.zeros((leaf_index.shape[0], 2, leaves), jnp.float32)
    return lax.fori_loop(0, length // width, one_block, empty)


def leaf_lookup(leaf_index, table):
    length = leaf_index.shape[1]
    width = math.gcd(length, 2048)
    labels = jnp.arange(table.shape[1], dtype=jnp.int32)

    def one_block(step, result):
        start = step * width
        part_leaf = lax.dynamic_slice_in_dim(leaf_index, start, width, 1)
        hits = part_leaf[:, None, :] == labels[None, :, None]
        picked = jnp.sum(jnp.where(hits, table[:, :, None], 0.0), axis=1)
        return lax.dynamic_update_slice_in_dim(result, picked, start, 1)

    empty = jnp.zeros(leaf_index.shape, jnp.float32)
    return lax.fori_loop(0, length // width, one_block, empty)


def on_device(predictions, leaf_index, events, tie_start):
    groups = predictions.shape[0]
    length = predictions.shape[1]
    backward, forward = tile_matrices(tie_start)
    weight = jnp.exp(predictions)
    local_risk = block_cumsum(weight, backward, True)
    block_total = local_risk[:, 0]
    zero_column = jnp.zeros((groups,), jnp.float32)
    later_total = prefix(block_total, "tm", add_values, zero_column, True)
    risk = local_risk + later_total[:, None]
    observed = events.astype(jnp.float32)
    inv_one = observed / risk
    inv_two = inv_one / risk
    local_one = block_cumsum(inv_one, forward, False)
    local_two = block_cumsum(inv_two, forward, False)
    totals_pair = (local_one[:, -1], local_two[:, -1])
    earlier_one, earlier_two = prefix(
        totals_pair, "tm", add_values, (zero_column, zero_column), False
    )
    accum_one = local_one + earlier_one[:, None]
    accum_two = local_two + earlier_two[:, None]
    gradient = weight * accum_one - observed
    hessian = weight * accum_one - weight * weight * accum_two
    stacked = jnp.stack([gradient, hessian]).astype(jnp.bfloat16).reshape(2, groups, 1, length)
    grad_hess = lax.all_to_all(stacked, "ep", split_axis=3, concat_axis=1, tiled=True)
    partial_value = leaf_partials(leaf_index, gradient, hessian, LEAVES)
    totals = lax.psum(partial_value, "tm")
    leaf_weights = -totals[:, 0] / (totals[:, 1] + 1.0)
    new_pred = predictions + leaf_lookup(leaf_index, leaf_weights)
    return (new_pred, leaf_weights, grad_hess)


def solution(mesh):
    placed = (P("ep", "tm"), P("ep", "tm"), P("ep", "tm"), P("tm"))
    return jax.shard_map(
        on_device,
        mesh=mesh,
        in_specs=placed,
        out_specs=(P("ep", "tm"), P("ep", None), P(None, None, "tm", "ep")),
        check_vma=False,
    )
```

profile of v0, /device:TPU:2, one launch (start us, length us, event | category | flops | bytes accessed | tf_op | source)
XLA Modules:
  0.0 666.5 jit_solution(1025747727024494581)
XLA Ops:
  0.6 6.2 exponential_bitcast_fusion.1
  7.2 2.9 copy.163
  10.1 1.1 bitcast_reduce_fusion.2
  12.6 10.0 %fusion.22 = f32[256,4,8,128]{3,2,1,0:T(8,128)S(1)} fusion(f32[4,256,8,128]{3,2,1,0:T(8,128)} %get-tuple-element.397, s32[256,128]{1,0:T(8,128)S(1)} %copy.130, f32[32,256]{0,1:T(8,128)S(1)} %copy.134), kind=kOutput, calls=%fused_computation.44 | convolution fusion | flops 1615855616 | bytes 8552448 | tf_op jit(solution)/shard_map/ebj,bji->ebi/dot_general | solution.py:44
  22.9 1.7 copy-done.1
  26.2 68.6 %all-reduce.1 = f32[1024]{0:T(1024)S(1)} all-reduce(f32[1024]{0:T(1024)S(1)} %dynamic-update-slice), channel_id=2, replica_groups=mesh['ep'=4,'tm'=32] {'tm'}, use_global_device_ids=true, to_apply=%add.1 | all-reduce | flops 1024 | bytes 8192
  94.9 1.3 while.52
  96.5 4.4 reduce_window_min.10
  101.0 9.3 %fusion.34 = (f32[4,8,256,128]{3,1,2,0:T(8,128)}, f32[4,256,8,128]{3,2,1,0:T(8,128)}, f32[4,256,8,128]{3,2,1,0:T(8,128)}, f32[4,8,256,128]{3,1,2,0:T(8,128)S(1)}) fusion(f32[32]{0:T(128)S(1)} %get-tuple-element.296, f32[256,4,8,128]{3,2,1,0:T(8,128)} %copy-done.1, s32[32,32768]{1,0:T(8,128)} %param.14), kind=kLoop, calls=%fused_computation.79 | loop fusion | flops 5242880 | bytes 25165952
  111.0 1.1 bitcast_reduce_fusion.1
  113.4 10.0 %fusion.21 = f32[256,4,8,128]{3,2,1,0:T(8,128)S(1)} fusion(f32[4,256,8,128]{3,2,1,0:T(8,128)} %get-tuple-element.394, s32[256,128]{1,0:T(8,128)S(1)} %copy.128, f32[32,256]{0,1:T(8,128)S(1)} %copy.139), kind=kOutput, calls=%fused_computation.42 | convolution fusion | flops 1615855616 | bytes 8552448 | tf_op jit(solution)/shard_map/ebj,bji->ebi/dot_general | solution.py:44
  123.7 1.8 copy-done
  125.7 1.4 copy-done.3
  127.8 1.1 bitcast_reduce_fusion
  130.0 10.0 %fusion.20 = f32[256,4,8,128]{3,2,1,0:T(8,128)S(1)} fusion(f32[4,256,8,128]{3,2,1,0:T(8,128)} %get-tuple-element.393, s32[256,128]{1,0:T(8,128)S(1)} %copy.128, f32[32,256]{0,1:T(8,128)S(1)} %copy.144), kind=kOutput, calls=%fused_computation.40 | convolution fusion | flops 1615855616 | bytes 8552448 | tf_op jit(solution)/shard_map/ebj,bji->ebi/dot_general | solution.py:44
  140.3 1.7 copy-done.2
  142.7 64.1 %all-reduce.4 = (f32[1024]{0:T(1024)S(1)}, f32[1024]{0:T(1024)S(1)}) all-reduce(f32[1024]{0:T(1024)S(1)} %dynamic-update-slice.1, f32[1024]{0:T(1024)S(1)} %dynamic-update-slice.2), channel_id=3, replica_groups=mesh['ep'=4,'tm'=32] {'tm'}, use_global_device_ids=true, to_apply=%add.2 | all-reduce | flops 2048 | bytes 16384
  206.9 10.2 %convert_bitcast_fusion = (bf16[1,32,1,32768]{3,1,2,0:T(8,128)(2,1)S(1)}, f32[32,32768]{1,0:T(8,128)}, bf16[1,32,1,32768]{3,1,2,0:T(8,128)(2,1)S(1)}, f32[32,32768]{1,0:T(8,128)}) fusion(f32[32]{0:T(128)S(1)} %get-tuple-element.298, f32[256,4,8,128]{3,2,1,0:T(8,128)} %copy-done.2, f32[32]{0:T(128)S(1)} %get-tuple-element.297, f32[256,4,8,128]{3,2,1,0:T(8,128)} %copy-done, ...), kind=kLoop, calls=%fused_computation.52 | loop fusion | flops 10485760 | bytes 29360384 | tf_op jit(solution)/shard_map/stack | solution.py:115
  217.1 2.4 pad_maximum_fusion
  219.5 33.0 %copy.146 = bf16[2,32,1,32768]{1,0,2,3:T(2,128)(2,1)} copy(bf16[2,32,1,32768]{3,1,2,0:T(8,128)(2,1)} %pad_maximum_fusion) | data formatting | bytes 8388608 | tf_op jit(solution)/shard_map/stack | solution.py:115
  252.5 19.2 %reshape.184 = bf16[4,2,262144]{2,1,0:T(2,128)(2,1)} reshape(bf16[32768,1,2,32]{3,2,1,0:T(2,128)(2,1)} %bitcast.143) | data formatting | bytes 8388608
  271.7 5.3 all-to-all-start
  277.1 117.7 %while.55 = (s32[]{:T(128)}, f32[32,2,64]{2,0,1:T(8,128)S(1)}, s32[32,32768]{1,0:T(8,128)}, f32[32,32768]{1,0:T(8,128)}, f32[32,32768]{1,0:T(8,128)}, /*index=5*/s32[]{:T(128)}, s32[]{:T(128)}, s32[]{:T(128)}, s32[]{:T(128)}) while((s32[]{:T(128)}, f32[32,2,64]{2,0,1:T(8,128)S(1)}, s32[32,32768]{1,0:T(8,128)}, ...), condition=%wide.region_18.19_spmd.clone, body=%wide.region_15.18_spmd.clone.sunk | while | flops 20979716 | bytes 2424997 | solution.py:73
  279.1 5.3 fusion.39
  284.4 1.1 constant_dynamic-slice_fusion.8
  286.5 5.3 fusion.39
  291.8 1.1 constant_dynamic-slice_fusion.8
  293.8 5.3 fusion.39
  301.2 5.3 fusion.39
  308.5 5.3 fusion.39
  315.9 5.3 fusion.39
  323.2 5.3 fusion.39
  330.6 5.3 fusion.39
  337.9 5.3 fusion.39
  345.3 5.3 fusion.39
  352.7 5.3 fusion.39
  360.0 5.3 fusion.39
  367.4 5.3 fusion.39
  374.7 5.3 fusion.39
  382.1 5.3 fusion.39
  389.4 5.3 fusion.39
  394.7 124.3 %psum.7 = f32[32,2,64]{2,0,1:T(8,128)S(1)} all-reduce(f32[32,2,64]{2,0,1:T(8,128)S(1)} %get-tuple-element.299), channel_id=1, replica_groups=mesh['ep'=4,'tm'=32] {'tm'}, use_global_device_ids=true, to_apply=%region_19.20 | all-reduce | flops 4096 | bytes 32768 | tf_op jit(solution)/shard_map/psum | solution.py:118
  519.1 2.3 broadcast_in_dim.125
  521.3 80.5 %while.54 = (s32[]{:T(128)}, f32[32,32768]{1,0:T(8,128)}, s32[32,32768]{1,0:T(8,128)}, f32[32,64]{1,0:T(8,128)S(1)}, s32[]{:T(128)}, /*index=5*/s32[]{:T(128)}, s32[]{:T(128)}, s32[]{:T(128)}) while((s32[]{:T(128)}, f32[32,32768]{1,0:T(8,128)}, s32[32,32768]{1,0:T(8,128)}, f32[32,64]{1,0:T(8,128)S(1)}, s32[]{:T(128)}, ...), condition=%wide.region_22.23_spmd.clone, body=%wide.region_20.22_spmd.clone.sunk | while | flops 12517382 | bytes 1581203 | solution.py:89
  522.3 3.3 select_reduce_fusion.2
  527.3 3.3 select_reduce_fusion.2
  532.4 3.3 select_reduce_fusion.2
  537.4 3.3 select_reduce_fusion.2
  542.4 3.3 select_reduce_fusion.2
  547.5 3.3 select_reduce_fusion.2
  552.5 3.3 select_reduce_fusion.2
  557.5 3.3 select_reduce_fusion.2
  562.6 3.3 select_reduce_fusion.2
  567.6 3.3 select_reduce_fusion.2
  572.6 3.3 select_reduce_fusion.2
  577.6 3.3 select_reduce_fusion.2
  582.7 3.3 select_reduce_fusion.2
  587.7 3.3 select_reduce_fusion.2
  592.7 3.3 select_reduce_fusion.2
  597.8 3.3 select_reduce_fusion.2
  601.8 5.9 add.165
  607.7 12.0 %reshape.185 = bf16[32768,1,2,32]{3,2,1,0:T(2,128)(2,1)} reshape(bf16[4,2,262144]{2,1,0:T(2,128)(2,1)} %all-to-all-done) | data formatting | bytes 8388608
  619.7 40.0 %copy.150 = bf16[2,32,1,4,8192]{4,3,1,0,2:T(4,128)(2,1)} copy(bf16[2,32,1,4,8192]{1,0,4,3,2:T(2,128)(2,1)} %bitcast.144) | data formatting | bytes 8388608 | tf_op jit(solution)/shard_map/all_to_all | solution.py:116
  659.8 6.5 copy.148
  (176 shorter events, 66.8 us)
Async XLA Ops:
  0.6 6.2 copy-start.5
  22.6 2.0 copy-start.1
  22.6 2.1 copy-start.6
  123.4 2.1 copy-start
  123.4 3.7 copy-start.3
  140.0 2.0 copy-start.2
  271.7 336.0 %all-to-all-start = ((bf16[4,2,262144]{2,1,0:T(2,128)(2,1)}), bf16[4,2,262144]{2,1,0:T(2,128)(2,1)}, u32[]{:S(2)}, u32[]{:S(2)}) async-start(bf16[4,2,262144]{2,1,0:T(2,128)(2,1)} %reshape.184), calls=%async_computation | async-start | bytes 8388608 | tf_op jit(solution)/shard_map/all_to_all | solution.py:116
  601.8 5.9 copy-start.4
where the time goes:
time: 677 us; the launch traced here: 666 us
  blocking collectives  257 us (38%)
  local copies, waits for them, and re-layouts  195 us (29%)
  other arithmetic  176 us (26%)
  matrix products  30 us (4%)
    unnamed x2, blocking collectives  133 us
    psum x1, blocking collectives, on_device(): totals = lax.psum(partial_value, 'tm')  124 us
    reduce_sum x16, other arithmetic, one_block(): gsum = jnp.sum(jnp.where(hits, part_grad[:, None, :], 0.0), axis=2)  84.3 us
    reduce_sum x16, other arithmetic, one_block(): picked = jnp.sum(jnp.where(hits, table[:, :, None], 0.0), axis=1)  53.2 us
    unnamed x27, local copies, waits for them, and re-layouts  49.8 us
    all_to_all x2, local copies, waits for them, and re-layouts, on_device(): lax.all_to_all(stacked, 'ep', split_axis=3, concat_axis=1, tiled=True)  46.5 us
    another operation x1, local copies, waits for them, and re-layouts, on_device(): jnp.stack([gradient, hessian]).astype(jnp.bfloat16)  33 us
    dynamic_slice x32, local copies, waits for them, and re-layouts, one_block(): part_leaf = lax.dynamic_slice_in_dim(leaf_index, start, width, 1)  31.1 us
  transfers between devices with their start and end apart: 1, of which 0 were waited for; matrix products, arithmetic and copies ran while one was open for 31% of the time, Pallas kernels for 0%

commit v1 on v0

--- a/solution.py
+++ b/solution.py
@@ -113,7 +113,20 @@
     gradient = weight * accum_one - observed
     hessian = weight * accum_one - weight * weight * accum_two
     stacked = jnp.stack([gradient, hessian]).astype(jnp.bfloat16).reshape(2, groups, 1, length)
-    grad_hess = lax.all_to_all(stacked, "ep", split_axis=3, concat_axis=1, tiled=True)
+    ways, here = (lax.axis_size("ep"), lax.axis_index("ep"))
+    width_2 = stacked.shape[3] // ways
+    shape = list(stacked.shape)
+    shape[3] = width_2
+    height = shape[1]
+    shape[1] = height * ways
+    grad_hess = jnp.zeros(shape, stacked.dtype)
+    for mask in range(ways):
+        part_2 = lax.dynamic_slice_in_dim(stacked, (here ^ mask) * width_2, width_2, axis=3)
+        if mask:
+            part_2 = lax.ppermute(part_2, "ep", [(d, d ^ mask) for d in range(ways)])
+        grad_hess = lax.dynamic_update_slice_in_dim(
+            grad_hess, part_2, (here ^ mask) * height, axis=1
+        )
     partial_value = leaf_partials(leaf_index, gradient, hessian, LEAVES)
     totals = lax.psum(partial_value, "tm")
     leaf_weights = -totals[:, 0] / (totals[:, 1] + 1.0)

time: 677 us -> 571 us (0.84)
  local copies, waits for them, and re-layouts: 195 us -> 88.3 us
    all_to_all x2 -> x0, local copies, waits for them, and re-layouts: 46.5 us -> none  [on_device(): lax.all_to_all(stacked, 'ep', split_axis=3, concat_axis=1, tiled=True)]
    unnamed x27, local copies, waits for them, and re-layouts: 49.8 us -> 15 us
    another operation x8 -> x7, local copies, waits for them, and re-layouts: 33.4 us -> 0.34 us  [the longest x1 33 us: on_device(): jnp.stack([gradient, hessian]).astype(jnp.bfloat16)]
  transfers between devices with their start and end apart: 1 -> 3, of which waited for: 0 -> 0; matrix products, arithmetic and copies ran while one was open for 31% -> 38% of each run, Pallas kernels for 0% -> 0%
where the time goes in v1:
time: 571 us; the launch traced here: 560 us
  blocking collectives  256 us (45%)
  other arithmetic  179 us (31%)
  local copies, waits for them, and re-layouts  88.3 us (15%)
  matrix products  30.1 us (5%)
    unnamed x2, blocking collectives  132 us
    psum x1, blocking collectives, on_device(): totals = lax.psum(partial_value, 'tm')  124 us
    reduce_sum x16, other arithmetic, one_block(): gsum = jnp.sum(jnp.where(hits, part_grad[:, None, :], 0.0), axis=2)  84.3 us
    reduce_sum x16, other arithmetic, one_block(): picked = jnp.sum(jnp.where(hits, table[:, :, None], 0.0), axis=1)  53.2 us
    dynamic_slice x32, local copies, waits for them, and re-layouts, one_block(): part_leaf = lax.dynamic_slice_in_dim(leaf_index, start, width, 1)  31.1 us
    dot_general x3, matrix products, block_cumsum(): jnp.einsum('ebj,bji->ebi', shaped, matrices, precision=lax.Precision.HIGH...  30.1 us
    dynamic_slice x16, local copies, waits for them, and re-layouts, one_block(): part_hess = lax.dynamic_slice_in_dim(hessian, start, width, 1)  17.1 us
    unnamed x27, local copies, waits for them, and re-layouts  15 us
  transfers between devices with their start and end apart: 3, of which 0 were waited for; matrix products, arithmetic and copies ran while one was open for 38% of the time, Pallas kernels for 0%

profile of v1, /device:TPU:2, one launch (start us, length us, event | category | flops | bytes accessed | tf_op | source)
XLA Modules:
  0.0 560.4 jit_solution(15467167268529573484)
XLA Ops:
  0.7 4.7 exponential_bitcast_fusion.1
  6.2 1.1 bitcast_reduce_fusion.2
  9.0 10.0 %fusion.22 = f32[256,4,8,128]{3,2,1,0:T(8,128)S(1)} fusion(f32[4,256,8,128]{3,2,1,0:T(8,128)} %get-tuple-element.391, s32[256,128]{1,0:T(8,128)S(1)} %copy.36, f32[32,256]{0,1:T(8,128)S(1)} %copy.40), kind=kOutput, calls=%fused_computation.51 | convolution fusion | flops 1615855616 | bytes 8552448 | tf_op jit(solution)/shard_map/ebj,bji->ebi/dot_general | solution.py:44
  19.3 1.7 copy-done.3
  22.7 68.6 %all-reduce.1 = f32[1024]{0:T(1024)S(1)} all-reduce(f32[1024]{0:T(1024)S(1)} %dynamic-update-slice), channel_id=2, replica_groups=mesh['ep'=4,'tm'=32] {'tm'}, use_global_device_ids=true, to_apply=%add.1 | all-reduce | flops 1024 | bytes 8192
  91.3 1.3 while.52
  92.6 9.4 %fusion.43 = (f32[4,8,256,128]{3,1,2,0:T(8,128)S(1)}, f32[4,256,8,128]{3,2,1,0:T(8,128)}, f32[4,256,8,128]{3,2,1,0:T(8,128)}, f32[4,8,256,128]{3,1,2,0:T(8,128)}) fusion(f32[32]{0:T(128)S(1)} %get-tuple-element.296, f32[256,4,8,128]{3,2,1,0:T(8,128)} %copy-done.3, s32[32,32768]{1,0:T(8,128)} %param.14), kind=kLoop, calls=%fused_computation.98 | loop fusion | flops 5242880 | bytes 25165952
  102.8 1.1 bitcast_reduce_fusion
  105.6 4.4 reduce_window_min.10
  110.1 10.0 %fusion.20 = f32[256,4,8,128]{3,2,1,0:T(8,128)S(1)} fusion(f32[4,256,8,128]{3,2,1,0:T(8,128)} %get-tuple-element.384, s32[256,128]{1,0:T(8,128)S(1)} %copy.34, f32[32,256]{0,1:T(8,128)S(1)} %copy.50), kind=kOutput, calls=%fused_computation.47 | convolution fusion | flops 1615855616 | bytes 8552448 | tf_op jit(solution)/shard_map/ebj,bji->ebi/dot_general | solution.py:44
  120.4 1.8 copy-done.1
  122.4 1.4 copy-done.4
  124.6 1.1 bitcast_reduce_fusion.1
  126.7 10.2 %fusion.21 = f32[256,4,8,128]{3,2,1,0:T(8,128)S(1)} fusion(f32[4,256,8,128]{3,2,1,0:T(8,128)} %get-tuple-element.385, s32[256,128]{1,0:T(8,128)S(1)} %copy.34, f32[32,256]{0,1:T(8,128)S(1)} %copy.45), kind=kOutput, calls=%fused_computation.49 | convolution fusion | flops 1615855616 | bytes 8552448 | tf_op jit(solution)/shard_map/ebj,bji->ebi/dot_general | solution.py:44
  137.2 1.7 copy-done.2
  139.5 63.7 %all-reduce.4 = (f32[1024]{0:T(1024)S(1)}, f32[1024]{0:T(1024)S(1)}) all-reduce(f32[1024]{0:T(1024)S(1)} %dynamic-update-slice.1, f32[1024]{0:T(1024)S(1)} %dynamic-update-slice.2), channel_id=3, replica_groups=mesh['ep'=4,'tm'=32] {'tm'}, use_global_device_ids=true, to_apply=%add.2 | all-reduce | flops 2048 | bytes 16384
  203.4 10.7 %convert_bitcast_fusion = (bf16[1,32,32768]{2,1,0:T(8,128)(2,1)S(1)}, f32[32,32768]{1,0:T(8,128)}, bf16[1,32,32768]{2,1,0:T(8,128)(2,1)}, f32[32,32768]{1,0:T(8,128)}) fusion(f32[32]{0:T(128)S(1)} %get-tuple-element.298, f32[256,4,8,128]{3,2,1,0:T(8,128)} %copy-done.1, f32[32]{0:T(128)S(1)} %get-tuple-element.297, f32[256,4,8,128]{3,2,1,0:T(8,128)} %copy-done.2, ...), kind=kLoop, calls=%fused_computation.59 | loop fusion | flops 10485760 | bytes 29360384 | tf_op jit(solution)/shard_map/stack | solution.py:115
  214.1 3.1 fusion.30
  217.8 2.4 collective-permute-start.1
  220.7 117.9 %while.55 = (s32[]{:T(128)}, f32[32,2,64]{2,0,1:T(8,128)S(1)}, s32[32,32768]{1,0:T(8,128)}, f32[32,32768]{1,0:T(8,128)}, f32[32,32768]{1,0:T(8,128)}, /*index=5*/s32[]{:T(128)}, s32[]{:T(128)}, s32[]{:T(128)}, s32[]{:T(128)}) while((s32[]{:T(128)}, f32[32,2,64]{2,0,1:T(8,128)S(1)}, s32[32,32768]{1,0:T(8,128)}, ...), condition=%wide.region_18.19_spmd.clone, body=%wide.region_15.18_spmd.clone.sunk | while | flops 20979716 | bytes 2424989 | solution.py:73
  220.9 1.1 constant_dynamic-slice_fusion.8
  223.0 5.3 fusion.48
  228.3 1.1 constant_dynamic-slice_fusion.8
  230.3 5.3 fusion.48
  235.6 1.1 constant_dynamic-slice_fusion.8
  237.7 5.3 fusion.48
  243.0 1.1 constant_dynamic-slice_fusion.8
  245.0 5.3 fusion.48
  250.3 1.1 constant_dynamic-slice_fusion.8
  252.4 5.3 fusion.48
  259.8 5.3 fusion.48
  267.1 5.3 fusion.48
  274.5 5.3 fusion.48
  281.8 5.3 fusion.48
  289.2 5.3 fusion.48
  296.5 5.3 fusion.48
  303.9 5.3 fusion.48
  311.2 5.3 fusion.48
  318.6 5.3 fusion.48
  326.0 5.3 fusion.48
  333.3 5.3 fusion.48
  338.6 123.8 %psum.7 = f32[32,2,64]{2,0,1:T(8,128)S(1)} all-reduce(f32[32,2,64]{2,0,1:T(8,128)S(1)} %get-tuple-element.299), channel_id=1, replica_groups=mesh['ep'=4,'tm'=32] {'tm'}, use_global_device_ids=true, to_apply=%region_19.20 | all-reduce | flops 4096 | bytes 32768 | tf_op jit(solution)/shard_map/psum | solution.py:131
  462.4 2.3 broadcast_in_dim.128
  464.7 80.5 %while.54 = (s32[]{:T(128)}, f32[32,32768]{1,0:T(8,128)}, s32[32,32768]{1,0:T(8,128)}, f32[32,64]{1,0:T(8,128)S(1)}, s32[]{:T(128)}, /*index=5*/s32[]{:T(128)}, s32[]{:T(128)}, s32[]{:T(128)}) while((s32[]{:T(128)}, f32[32,32768]{1,0:T(8,128)}, s32[32,32768]{1,0:T(8,128)}, f32[32,64]{1,0:T(8,128)S(1)}, s32[]{:T(128)}, ...), condition=%wide.region_22.23_spmd.clone, body=%wide.region_20.22_spmd.clone.sunk | while | flops 12517382 | bytes 1581195 | solution.py:89
  465.6 3.3 select_reduce_fusion.2
  470.7 3.3 select_reduce_fusion.2
  475.7 3.3 select_reduce_fusion.2
  480.7 3.3 select_reduce_fusion.2
  485.8 3.3 select_reduce_fusion.2
  490.8 3.3 select_reduce_fusion.2
  495.8 3.3 select_reduce_fusion.2
  500.9 3.3 select_reduce_fusion.2
  505.9 3.3 select_reduce_fusion.2
  510.9 3.3 select_reduce_fusion.2
  515.9 3.3 select_reduce_fusion.2
  521.0 3.3 select_reduce_fusion.2
  526.0 3.3 select_reduce_fusion.2
  531.0 3.3 select_reduce_fusion.2
  536.1 3.3 select_reduce_fusion.2
  541.1 3.3 select_reduce_fusion.2
  545.1 2.5 broadcast_in_dim.135
  548.7 5.9 %add.189 = f32[32,32768]{1,0:T(8,128)} add(f32[32,32768]{1,0:T(8,128)} %param.12, f32[32,32768]{1,0:T(8,128)} %get-tuple-element.300) | non-fusion elementwise | flops 1048576 | bytes 12582912 | tf_op jit(solution)/shard_map/add | solution.py:133
  554.6 2.3 constant_dynamic-update-slice_fusion.3
  556.8 2.3 constant_dynamic-update-slice_fusion.1
  (182 shorter events, 67.8 us)
Async XLA Ops:
  6.1 2.5 copy-start.6
  19.0 2.0 copy-start.3
  19.0 2.1 copy-start.7
  120.1 2.1 copy-start.1
  120.1 3.7 copy-start.4
  136.9 2.0 copy-start.2
  217.2 337.3 %collective-permute-start = (bf16[2,32,1,8192]{3,1,2,0:T(8,128)(2,1)}, bf16[2,32,1,8192]{3,1,2,0:T(8,128)(2,1)}, u32[]{:S(2)}, u32[]{:S(2)}) collective-permute-start(bf16[2,32,1,8192]{3,1,2,0:T(8,128)(2,1)} %get-tuple-element.388), channel_id=1, source_target_pairs={{0,32},{32,0},{64,96},{96,64},{1,33},{33,1},{65,97},{97,65},{2,34}... | collective-permute-start | bytes 3145736 | tf_op jit(solution)/shard_map/ppermute | solution.py:126
  217.8 339.1 %collective-permute-start.1 = (bf16[2,32,1,8192]{3,1,2,0:T(8,128)(2,1)}, bf16[2,32,1,8192]{3,1,2,0:T(8,128)(2,1)}, u32[]{:S(2)}, u32[]{:S(2)}) collective-permute-start(bf16[2,32,1,8192]{3,1,2,0:T(8,128)(2,1)} %get-tuple-element.389), channel_id=1, source_target_pairs={{0,64},{32,96},{64,0},{96,32},{1,65},{33,97},{65,1},{97,33},{2,66}... | collective-permute-start | bytes 3145736 | tf_op jit(solution)/shard_map/ppermute | solution.py:126
  220.2 338.9 %collective-permute-start.2 = (bf16[2,32,1,8192]{3,1,2,0:T(8,128)(2,1)}, bf16[2,32,1,8192]{3,1,2,0:T(8,128)(2,1)S(1)}, u32[]{:S(2)}, u32[]{:S(2)}) collective-permute-start(bf16[2,32,1,8192]{3,1,2,0:T(8,128)(2,1)} %get-tuple-element.387), channel_id=1, source_target_pairs={{0,96},{32,64},{64,32},{96,0},{1,97},{33,65},{65,33},{97,1},{2,98}... | collective-permute-start | bytes 3145736 | tf_op jit(solution)/shard_map/ppermute | solution.py:126
  545.1 3.5 copy-start.5
  545.1 2.5 copy-start
